TPU v7x, 32 devices: a whole 2x2x4 slice. The times are simulated.
32 devices in a mesh: cube: 4 (over z), front: 8 (over y, x, core).
Axes of the slice: x: 2, y: 2, z: 4, core: 2. Of those that a mesh axis runs over, the one named last changes fastest.
Arguments:
- right_sides: float32 [3, 4, 512, 128], P(None, 'cube', 'front'), may hold values from -6 to 6
- inverse_leaf: float32 [4, 512, 512], P('cube', 'front'), may hold values from -2 to 2, as said below
- inverse_mid: float32 [4, 512, 1024], P('cube', 'front'), may hold values from -2 to 2, as said below
- inverse_top: float32 [4, 512, 2048], P('cube', 'front'), may hold values from -2 to 2, as said below
- coupling_mid: float32 [4, 512, 1024], P('cube', 'front'), may hold values from -0.25 to 0.25
- coupling_top: float32 [4, 512, 2048], P('cube', 'front'), may hold values from -0.1875 to 0.1875
- pattern_mid: int32 [4, 8, 16], P('cube', 'front'), may hold values 0 or 1
- pattern_top: int32 [4, 8, 32], P('cube', 'front'), may hold values 0 or 1
Outputs:
- solution: float32 [3, 4, 512, 128], P(None, 'cube', 'front')
Inputs may be any that keep to these rules, and one draw needn't show every extreme that they name: `inverse_leaf`: each block is the inverse of a lower triangular diagonal block: zero above the diagonal of the separator's row order, diagonal 1 to 2. `inverse_mid`: as inverse_leaf. `inverse_top`: as inverse_leaf.
All inputs are finite; a program needn't handle non-finite values. No bound on the sum of `pattern_mid` or of `pattern_top` on one device may be relied on, other than what follows from the above.
Results may differ from a plain program's by a relative error of at most 0.00013.
Values sent between devices are 32-bit elements; how exact they have to be, the bound alone decides.
No kernel may reach another device: no remote copies, remote signals or barrier semaphores. Data moves between devices by JAX's collectives and lax.ppermute only.
A program may use at most 64 MiB of HBM per device.

v0:
```python
import jax
import jax.numpy as jnp
from jax import lax
from jax.sharding import PartitionSpec as P

TILE = 64


def from_partner(value, axis, distance):
    mask = 2**distance
    pairs = [(source, source ^ mask) for source in range(lax.axis_size(axis))]
    return lax.ppermute(value, axis, pairs)


def masked(coupling, pattern):
    keep_rows = jnp.repeat(pattern[0], TILE, axis=0)
    keep_all = jnp.repeat(keep_rows, TILE, axis=1)
    return coupling[0] * keep_all.astype(jnp.float32)


def members_of(local_rows, count, cube_pos):
    if count == 1:
        return local_rows[None]
    stacked = local_rows[None]
    for bit_index in range(count.bit_length() - 1):
        partner = from_partner(stacked, "cube", bit_index)
        upper = cube_pos // 2**bit_index % 2
        stacked = jnp.where(
            upper == 0,
            jnp.concatenate([stacked, partner], 0),
            jnp.concatenate([partner, stacked], 0),
        )
    return stacked


def gathered_product(matrix, stacked):
    count = stacked.shape[0]
    height = matrix.shape[0]
    member_width = matrix.shape[1] // count
    shaped = matrix.reshape(height, count, member_width)
    return jnp.einsum(
        "rms,msn->rn",
        shaped,
        lax.all_gather(stacked, "front", axis=1, tiled=True),
        precision=lax.Precision.HIGHEST,
        preferred_element_type=jnp.float32,
    )


def spread_back(matrix, local_rows, count, cube_pos):
    height = matrix.shape[0]
    member_width = matrix.shape[1] // count
    shaped = matrix.reshape(height, count, member_width)
    summed = lax.psum_scatter(
        jnp.einsum(
            "rms,rn->smn",
            shaped,
            local_rows,
            precision=lax.Precision.HIGHEST,
            preferred_element_type=jnp.float32,
        ),
        "front",
        scatter_dimension=0,
        tiled=True,
    )
    if count == 1:
        return summed[:, 0]
    stacked = summed
    for bit_index in reversed(range(count.bit_length() - 1)):
        half_size = stacked.shape[1] // 2
        upper = cube_pos // 2**bit_index % 2
        kept = lax.dynamic_slice_in_dim(stacked, upper * half_size, half_size, 1)
        outgoing = lax.dynamic_slice_in_dim(stacked, (1 - upper) * half_size, half_size, 1)
        stacked = kept + from_partner(outgoing, "cube", bit_index)
    return stacked[:, 0]


def local(
    right_sides,
    inverse_leaf,
    inverse_mid,
    inverse_top,
    coupling_mid,
    coupling_top,
    pattern_mid,
    pattern_top,
):
    cube_pos = lax.axis_index("cube")
    block_mid = masked(coupling_mid, pattern_mid)
    block_top = masked(coupling_top, pattern_top)
    inv_leaf = inverse_leaf[0]
    inv_mid = inverse_mid[0]
    inv_top = inverse_top[0]
    sides = right_sides[:, 0]
    solved_leaf = gathered_product(inv_leaf, members_of(sides[0], 1, cube_pos))
    update_mid = gathered_product(block_mid, members_of(solved_leaf, 2, cube_pos))
    solved_mid = gathered_product(inv_mid, members_of(sides[1] - update_mid, 2, cube_pos))
    update_top = gathered_product(block_top, members_of(solved_mid, 4, cube_pos))
    solved_top = gathered_product(inv_top, members_of(sides[2] - update_top, 4, cube_pos))
    back_top = spread_back(inv_top, solved_top, 4, cube_pos)
    carry_mid = spread_back(block_top, back_top, 4, cube_pos)
    back_mid = spread_back(inv_mid, solved_mid - carry_mid, 2, cube_pos)
    carry_leaf = spread_back(block_mid, back_mid, 2, cube_pos)
    back_leaf = spread_back(inv_leaf, solved_leaf - carry_leaf, 1, cube_pos)
    result = jnp.stack([back_leaf, back_mid, back_top])
    return result[:, None]


def solution(mesh):
    return jax.shard_map(
        local,
        mesh=mesh,
        in_specs=(
            P(None, "cube", "front", None),
            P("cube", "front", None),
            P("cube", "front", None),
            P("cube", "front", None),
            P("cube", "front", None),
            P("cube", "front", None),
            P("cube", "front", None),
            P("cube", "front", None),
        ),
        out_specs=P(None, "cube", "front", None),
        check_vma=False,
    )
```

profile of v0, /device:TPU:0, one launch (start us, length us, event | category | flops | bytes accessed | tf_op | source)
XLA Modules:
  0.0 384.1 jit_solution(2500228545821510919)
XLA Ops:
  7.4 10.8 %all-gather = f32[1,1,512,128]{3,2,1,0:T(8,128)S(1)} all-gather(f32[1,1,64,128]{3,2,1,0:T(8,128)S(1)} %slice-done), channel_id=2, replica_groups=mesh['cube'=4,'front'=8] {'front'}, dimensions={2}, use_global_device_ids=true | all-gather | bytes 294912 | tf_op jit(solution)/shard_map/all_gather | solution.py:44
  18.4 1.6 collective-permute-start
  20.6 1.8 collective-permute-done
  22.4 10.0 %all_gather.16 = f32[2,512,128]{2,1,0:T(8,128)S(1)} all-gather(f32[2,64,128]{2,1,0:T(8,128)S(1)} %maximum_select_fusion.2), channel_id=1, replica_groups=mesh['cube'=4,'front'=8] {'front'}, dimensions={1}, use_global_device_ids=true | all-gather | bytes 589824 | tf_op jit(solution)/shard_map/all_gather | solution.py:44
  32.9 1.6 collective-permute-start.1
  34.7 2.1 collective-permute-done.1
  36.8 8.9 %all_gather.17 = f32[2,512,128]{2,1,0:T(8,128)S(1)} all-gather(f32[2,64,128]{2,1,0:T(8,128)S(1)} %maximum_select_fusion.3), channel_id=1, replica_groups=mesh['cube'=4,'front'=8] {'front'}, dimensions={1}, use_global_device_ids=true | all-gather | bytes 589824 | tf_op jit(solution)/shard_map/all_gather | solution.py:44
  47.8 2.3 collective-permute-done.2
  50.2 2.7 collective-permute-start.3
  52.8 2.6 collective-permute-done.3
  57.0 23.5 %all-gather.4.cloned.1.call-done = f32[4,512,128]{2,1,0:T(8,128)} async-done(((f32[4,64,128]{2,1,0:T(8,128)}), f32[4,512,128]{2,1,0:T(8,128)}) %all-gather.4.cloned.1.call-update) | async-done | bytes 1048592 | tf_op jit(solution)/shard_map/all_gather | solution.py:44
  80.5 2.1 fusion.1
  84.1 2.4 collective-permute-done.4
  86.6 2.5 collective-permute-start.5
  89.0 2.8 collective-permute-done.5
  92.9 23.8 %all-gather.6.cloned.1.call-done = f32[4,512,128]{2,1,0:T(8,128)} async-done(((f32[4,64,128]{2,1,0:T(8,128)}), f32[4,512,128]{2,1,0:T(8,128)}) %all-gather.6.cloned.1.call-update) | async-done | bytes 1048592 | tf_op jit(solution)/shard_map/all_gather | solution.py:44
  116.7 2.1 fusion.5
  123.1 54.9 %all-reduce.5.cloned.1.call-done = f32[512,4,128]{2,1,0:T(4,128)} async-done(((f32[512,4,128]{2,1,0:T(4,128)}), f32[512,4,128]{2,1,0:T(4,128)}) %all-reduce.5.cloned.1.call-update) | async-done | bytes 1048592
  179.0 2.4 collective-permute-start.6
  181.5 2.7 collective-permute-done.6
  187.1 2.1 collective-permute-done.7
  189.2 2.8 convolution_bitcast_fusion
  192.3 35.8 %reduce-scatter.4.cloned.1.call-done = f32[64,4,128]{2,0,1:T(8,128)} async-done(((f32[512,4,128]{2,0,1:T(8,128)}), f32[64,4,128]{2,0,1:T(8,128)}) %reduce-scatter.4.cloned.1.call-update) | async-done | bytes 131088 | tf_op jit(solution)/shard_map/reduce_scatter | solution.py:54
  229.1 2.4 collective-permute-start.8
  231.5 2.9 collective-permute-done.8
  235.8 2.6 collective-permute-done.9
  240.3 55.3 %all-reduce.7.cloned.1.call-done = f32[512,2,128]{2,1,0:T(2,128)} async-done(((f32[512,2,128]{2,1,0:T(2,128)}), f32[512,2,128]{2,1,0:T(2,128)}) %all-reduce.7.cloned.1.call-update) | async-done | bytes 524304
  298.3 2.3 collective-permute-done.10
  300.5 1.8 convolution_bitcast_fusion.2
  302.4 33.5 %reduce-scatter.6.cloned.1.call-done = f32[64,2,128]{2,0,1:T(8,128)} async-done(((f32[512,2,128]{2,0,1:T(8,128)}), f32[64,2,128]{2,0,1:T(8,128)}) %reduce-scatter.6.cloned.1.call-update) | async-done | bytes 65552 | tf_op jit(solution)/shard_map/reduce_scatter | solution.py:54
  338.3 2.4 collective-permute-done.11
  342.0 33.8 %reduce-scatter.8.cloned.1.call-done = f32[64,1,128]{2,1,0:T(1,128)} async-done(((f32[512,1,128]{2,1,0:T(1,128)}), f32[64,1,128]{2,1,0:T(1,128)}) %reduce-scatter.8.cloned.1.call-update) | async-done | bytes 32784 | tf_op jit(solution)/shard_map/reduce_scatter | solution.py:54
  (93 shorter events, 28.4 us)
Async XLA Ops:
  6.5 11.6 %copy-start = (f32[1,64,512]{2,1,0:T(8,128)S(1)}, f32[1,64,512]{2,1,0:T(8,128)}, u32[]{:S(2)}) copy-start(f32[1,64,512]{2,1,0:T(8,128)} %param.9) | copy-start | bytes 393220
  6.5 0.8 slice-start
  6.5 73.9 %all-gather.4.cloned.1.call-start = ((), (), s32[]{:S(2)}) async-start(), calls=%async_computation.3 | async-start | bytes 1179648 | tf_op jit(solution)/shard_map/all_gather | solution.py:44
  18.1 2.0 copy-start.2
  18.4 1.7 copy-start.9
  18.4 4.0 %collective-permute-start = (f32[1,64,128]{2,1,0:T(8,128)S(1)}, f32[1,64,128]{2,1,0:T(8,128)S(1)}, u32[]{:S(2)}, u32[]{:S(2)}) collective-permute-start(f32[1,64,128]{2,1,0:T(8,128)S(1)} %bitcast.93), channel_id=1, source_target_pairs={{0,8},{8,0},{16,24},{24,16},{1,9},{9,1},{17,25},{25,17},{2,10},{10... | collective-permute-start | bytes 98312 | tf_op jit(solution)/shard_map/ppermute | solution.py:12
  22.4 10.0 %copy-start.6 = (f32[3,1,64,128]{3,2,1,0:T(8,128)S(1)}, f32[3,1,64,128]{3,2,1,0:T(8,128)}, u32[]{:S(2)}) copy-start(f32[3,1,64,128]{3,2,1,0:T(8,128)} %param.8) | copy-start | bytes 294916
  32.4 2.1 copy-start.4
  32.9 4.0 %collective-permute-start.1 = (f32[1,64,128]{2,1,0:T(8,128)S(1)}, f32[1,64,128]{2,1,0:T(8,128)S(1)}, u32[]{:S(2)}, u32[]{:S(2)}) collective-permute-start(f32[1,64,128]{2,1,0:T(8,128)S(1)} %fusion.3), channel_id=1, source_target_pairs={{0,8},{8,0},{16,24},{24,16},{1,9},{9,1},{17,25},{25,17},{2,10},{10... | collective-permute-start | bytes 98312 | tf_op jit(solution)/shard_map/ppermute | solution.py:12
  45.7 10.4 %copy-start.1 = (f32[1,64,2048]{2,1,0:T(8,128)S(1)}, f32[1,64,2048]{2,1,0:T(8,128)}, u32[]{:S(2)}) copy-start(f32[1,64,2048]{2,1,0:T(8,128)} %param.13) | copy-start | bytes 1572868
  46.2 4.0 %collective-permute-start.2 = (f32[1,64,128]{2,1,0:T(8,128)S(1)}, f32[1,64,128]{2,1,0:T(8,128)S(1)}, u32[]{:S(2)}, u32[]{:S(2)}) collective-permute-start(f32[1,64,128]{2,1,0:T(8,128)S(1)} %bitcast.89), channel_id=1, source_target_pairs={{0,8},{8,0},{16,24},{24,16},{1,9},{9,1},{17,25},{25,17},{2,10},{10... | collective-permute-start | bytes 98312 | tf_op jit(solution)/shard_map/ppermute | solution.py:12
  50.2 5.2 %collective-permute-start.3 = (f32[2,64,128]{2,1,0:T(8,128)S(1)}, f32[2,64,128]{2,1,0:T(8,128)S(1)}, u32[]{:S(2)}, u32[]{:S(2)}) collective-permute-start(f32[2,64,128]{2,1,0:T(8,128)S(1)} %maximum_select_fusion.4), channel_id=1, source_target_pairs={{0,16},{8,24},{16,0},{24,8},{1,17},{9,25},{17,1},{25,9},{2,18},{10... | collective-permute-start | bytes 196616 | tf_op jit(solution)/shard_map/ppermute | solution.py:12
  56.1 0.7 copy-start.8
  56.1 60.6 %all-gather.6.cloned.1.call-start = ((), (), s32[]{:S(2)}) async-start(), calls=%async_computation.4 | async-start | bytes 1179648 | tf_op jit(solution)/shard_map/all_gather | solution.py:44
  82.5 10.0 %copy-start.3 = (f32[1,64,2048]{2,1,0:T(8,128)S(1)}, f32[1,64,2048]{2,1,0:T(8,128)}, u32[]{:S(2)}) copy-start(f32[1,64,2048]{2,1,0:T(8,128)} %param.11) | copy-start | bytes 1572868
  82.6 4.0 %collective-permute-start.4 = (f32[1,64,128]{2,1,0:T(8,128)S(1)}, f32[1,64,128]{2,1,0:T(8,128)S(1)}, u32[]{:S(2)}, u32[]{:S(2)}) collective-permute-start(f32[1,64,128]{2,1,0:T(8,128)S(1)} %fusion.1), channel_id=1, source_target_pairs={{0,8},{8,0},{16,24},{24,16},{1,9},{9,1},{17,25},{25,17},{2,10},{10... | collective-permute-start | bytes 98312 | tf_op jit(solution)/shard_map/ppermute | solution.py:12
  86.6 5.2 %collective-permute-start.5 = (f32[2,64,128]{2,1,0:T(8,128)S(1)}, f32[2,64,128]{2,1,0:T(8,128)S(1)}, u32[]{:S(2)}, u32[]{:S(2)}) collective-permute-start(f32[2,64,128]{2,1,0:T(8,128)S(1)} %maximum_select_fusion.5), channel_id=1, source_target_pairs={{0,16},{8,24},{16,0},{24,8},{1,17},{9,25},{17,1},{25,9},{2,18},{10... | collective-permute-start | bytes 196616 | tf_op jit(solution)/shard_map/ppermute | solution.py:12
  92.5 85.6 %all-reduce.5.cloned.1.call-start = ((), (), s32[]{:S(2)}) async-start(), calls=%async_computation.8 | async-start | bytes 2097152
  121.2 107.0 %reduce-scatter.4.cloned.1.call-start = ((), (), s32[]{:S(2)}) async-start(), calls=%async_computation.5 | async-start | bytes 1179648 | tf_op jit(solution)/shard_map/reduce_scatter | solution.py:54
  121.2 0.7 copy-start.10
  179.0 5.2 %collective-permute-start.6 = (f32[64,2,128]{2,1,0:T(2,128)S(1)}, f32[64,2,128]{2,1,0:T(2,128)S(1)}, u32[]{:S(2)}, u32[]{:S(2)}) collective-permute-start(f32[64,2,128]{2,1,0:T(2,128)S(1)} %constant_dynamic-slice_fusion.6), channel_id=1, source_target_pairs={{0,16},{8,24},{16,0},{24,8},{1,17},{9,25},{17,1},{25,9},{2,18},{10... | collective-permute-start | bytes 196616 | tf_op jit(solution)/shard_map/ppermute | solution.py:12
  185.2 4.0 %collective-permute-start.7 = (f32[64,1,128]{2,1,0:T(1,128)S(1)}, f32[64,1,128]{2,1,0:T(1,128)S(1)}, u32[]{:S(2)}, u32[]{:S(2)}) collective-permute-start(f32[64,1,128]{2,1,0:T(1,128)S(1)} %constant_dynamic-slice_fusion.5), channel_id=1, source_target_pairs={{0,8},{8,0},{16,24},{24,16},{1,9},{9,1},{17,25},{25,17},{2,10},{10... | collective-permute-start | bytes 98312 | tf_op jit(solution)/shard_map/ppermute | solution.py:12
  192.1 103.5 %all-reduce.7.cloned.1.call-start = ((), (), s32[]{:S(2)}) async-start(), calls=%async_computation.9 | async-start | bytes 1048576
  228.2 6.2 %copy-start.5 = (f32[64,4,128]{2,0,1:T(8,128)S(1)}, f32[64,4,128]{2,0,1:T(8,128)}, u32[]{:S(2)}) copy-start(f32[64,4,128]{2,0,1:T(8,128)} %reduce-scatter.4.cloned.1.call-done) | copy-start | bytes 393220
  229.1 5.3 %collective-permute-start.8 = (f32[64,2,128]{2,0,1:T(8,128)S(1)}, f32[64,2,128]{2,0,1:T(8,128)S(1)}, u32[]{:S(2)}, u32[]{:S(2)}) collective-permute-start(f32[64,2,128]{2,0,1:T(8,128)S(1)} %constant_dynamic-slice_fusion.4), channel_id=1, source_target_pairs={{0,16},{8,24},{16,0},{24,8},{1,17},{9,25},{17,1},{25,9},{2,18},{10... | collective-permute-start | bytes 196616 | tf_op jit(solution)/shard_map/ppermute | solution.py:12
  234.4 4.0 %collective-permute-start.9 = (f32[64,1,128]{2,0,1:T(8,128)S(1)}, f32[64,1,128]{2,0,1:T(8,128)S(1)}, u32[]{:S(2)}, u32[]{:S(2)}) collective-permute-start(f32[64,1,128]{2,0,1:T(8,128)S(1)} %constant_dynamic-slice_fusion.3), channel_id=1, source_target_pairs={{0,8},{8,0},{16,24},{24,16},{1,9},{9,1},{17,25},{25,17},{2,10},{10... | collective-permute-start | bytes 98312 | tf_op jit(solution)/shard_map/ppermute | solution.py:12
  240.0 95.9 %reduce-scatter.6.cloned.1.call-start = ((), (), s32[]{:S(2)}) async-start(), calls=%async_computation.6 | async-start | bytes 589824 | tf_op jit(solution)/shard_map/reduce_scatter | solution.py:54
  296.6 4.0 %collective-permute-start.10 = (f32[64,1,128]{2,0,1:T(8,128)S(1)}, f32[64,1,128]{2,0,1:T(8,128)S(1)}, u32[]{:S(2)}, u32[]{:S(2)}) collective-permute-start(f32[64,1,128]{2,0,1:T(8,128)S(1)} %bitcast.97), channel_id=1, source_target_pairs={{0,8},{8,0},{16,24},{24,16},{1,9},{9,1},{17,25},{25,17},{2,10},{10... | collective-permute-start | bytes 98312 | tf_op jit(solution)/shard_map/ppermute | solution.py:12
  302.4 73.5 %reduce-scatter.8.cloned.1.call-start = ((), (), s32[]{:S(2)}) async-start(), calls=%async_computation.7 | async-start | bytes 294912 | tf_op jit(solution)/shard_map/reduce_scatter | solution.py:54
  335.9 4.8 %copy-start.7 = (f32[64,2,128]{2,0,1:T(8,128)S(1)}, f32[64,2,128]{2,0,1:T(8,128)}, u32[]{:S(2)}) copy-start(f32[64,2,128]{2,0,1:T(8,128)} %reduce-scatter.6.cloned.1.call-done) | copy-start | bytes 196612
  336.8 3.9 %collective-permute-start.11 = (f32[64,1,128]{2,0,1:T(8,128)S(1)}, f32[64,1,128]{2,0,1:T(8,128)S(1)}, u32[]{:S(2)}, u32[]{:S(2)}) collective-permute-start(f32[64,1,128]{2,0,1:T(8,128)S(1)} %constant_dynamic-slice_fusion.1), channel_id=1, source_target_pairs={{0,8},{8,0},{16,24},{24,16},{1,9},{9,1},{17,25},{25,17},{2,10},{10... | collective-permute-start | bytes 98312 | tf_op jit(solution)/shard_map/ppermute | solution.py:12
Sparse Core Ops, SparseCore 0:
  56.2 24.2 all-gather.3
  92.6 24.0 all-gather.5
  121.3 56.7 all-reduce.4
  192.2 35.9 reduce-scatter.3
  240.2 55.3 all-reduce.6
  302.5 33.4 reduce-scatter.5
  342.1 33.6 reduce-scatter.7
where the time goes:
time: 385 us; the launch traced here: 384 us
  waiting for transfers between devices  290 us (75%)
  blocking collectives  29.6 us (8%)
  starting transfers between devices  22.7 us (6%)
  between operations  14.4 us (4%)
  matrix products  12.1 us (3%)
  local copies, waits for them, and re-layouts  11.6 us (3%)
  other arithmetic  3.85 us (1%)
    unnamed x9, waiting for transfers between devices  110 us
    reduce_scatter x3, waiting for transfers between devices, spread_back(): lax.psum_scatter(jnp.einsum('rms,rn->smn', shaped, local_rows, precision=...  103 us
    all_gather x2, waiting for transfers between devices, gathered_product(): lax.all_gather(stacked, 'front', axis=1, tiled=True)  47.3 us
    all_gather x3, blocking collectives, gathered_product(): lax.all_gather(stacked, 'front', axis=1, tiled=True)  29.6 us
    ppermute x12, waiting for transfers between devices, from_partner(): return lax.ppermute(value, axis, pairs)  28.9 us
    ppermute x12, starting transfers between devices, from_partner(): return lax.ppermute(value, axis, pairs)  22.3 us
  transfers between devices with their start and end apart: 19, of which 19 were waited for; matrix products, arithmetic and copies ran while one was open for 1% of the time, Pallas kernels for 0%

commit v1 on v0

--- a/solution.py
+++ b/solution.py
@@ -4,6 +4,22 @@
 from jax.sharding import PartitionSpec as P
 
 TILE = 64
+
+
+def product_in_turn(x, axis, dim, term):
+    size, index, extent = (lax.axis_size(axis), lax.axis_index(axis), x.shape[dim])
+    ahead = [(i, (i + 1) % size) for i in range(size)]
+    behind = [(i, (i - 1) % size) for i in range(size)]
+    half = size // 2
+    from_left = from_right = x
+    total = term(x, index * extent)
+    for step in range(1, half + 1):
+        from_left = lax.ppermute(from_left, axis, ahead)
+        if step < size - half:
+            from_right = lax.ppermute(from_right, axis, behind)
+            total = total + term(from_right, (index + step) % size * extent)
+        total = total + term(from_left, (index - step) % size * extent)
+    return total
 
 
 def from_partner(value, axis, distance):
@@ -38,12 +54,17 @@
     height = matrix.shape[0]
     member_width = matrix.shape[1] // count
     shaped = matrix.reshape(height, count, member_width)
-    return jnp.einsum(
-        "rms,msn->rn",
-        shaped,
-        lax.all_gather(stacked, "front", axis=1, tiled=True),
-        precision=lax.Precision.HIGHEST,
-        preferred_element_type=jnp.float32,
+    return product_in_turn(
+        stacked,
+        "front",
+        1,
+        lambda part, offset: jnp.einsum(
+            "rms,msn->rn",
+            lax.dynamic_slice_in_dim(shaped, offset, part.shape[1], axis=2),
+            part,
+            precision=lax.Precision.HIGHEST,
+            preferred_element_type=jnp.float32,
+        ),
     )
 
 

time: 385 us -> 401 us (1.042)
  starting transfers between devices: 22.7 us -> 63.2 us
  blocking collectives: 29.6 us -> 0 us
  matrix products: 12.1 us -> 20.1 us
    all_gather x2 -> x0, waiting for transfers between devices: 47.3 us -> none  [gathered_product(): lax.all_gather(stacked, 'front', axis=1, tiled=True)]
    ppermute x0 -> x35, waiting for transfers between devices: none -> 45 us  [the longest x20 41 us: product_in_turn(): from_left = lax.ppermute(from_left, axis, ahead)]
    ppermute x0 -> x35, starting transfers between devices: none -> 41.3 us  [the longest x15 41 us: product_in_turn(): from_right = lax.ppermute(from_right, axis, behind)]
    all_gather x3 -> x0, blocking collectives: 29.6 us -> none  [gathered_product(): lax.all_gather(stacked, 'front', axis=1, tiled=True)]
    dot_general x5 -> x40, matrix products: 5.35 us -> 13.4 us  [gathered_product(): jnp.einsum('rms,msn->rn', lax.dynamic_slice_in_dim(shaped, offset, part.s...]
    unnamed x9 -> x7, waiting for transfers between devices: 110 us -> 110 us
  transfers between devices with their start and end apart: 19 -> 52, of which waited for: 19 -> 46; matrix products, arithmetic and copies ran while one was open for 1% -> 4% of each run, Pallas kernels for 0% -> 0%
where the time goes in v1:
time: 401 us; the launch traced here: 400 us
  waiting for transfers between devices  288 us (72%)
  starting transfers between devices  63.2 us (16%)
  matrix products  20.1 us (5%)
  between operations  14.6 us (4%)
  local copies, waits for them, and re-layouts  11.6 us (3%)
    unnamed x7, waiting for transfers between devices  110 us
    reduce_scatter x3, waiting for transfers between devices, spread_back(): lax.psum_scatter(jnp.einsum('rms,rn->smn', shaped, local_rows, precision=...  103 us
    ppermute x20, waiting for transfers between devices, product_in_turn(): from_left = lax.ppermute(from_left, axis, ahead)  41 us
    ppermute x15, starting transfers between devices, product_in_turn(): from_right = lax.ppermute(from_right, axis, behind)  41 us
    ppermute x12, waiting for transfers between devices, from_partner(): return lax.ppermute(value, axis, pairs)  29.5 us
    ppermute x12, starting transfers between devices, from_partner(): return lax.ppermute(value, axis, pairs)  21.7 us
    dot_general x40, matrix products, gathered_product(): jnp.einsum('rms,msn->rn', lax.dynamic_slice_in_dim(shaped, offset, part.s...  13.4 us
  transfers between devices with their start and end apart: 52, of which 46 were waited for; matrix products, arithmetic and copies ran while one was open for 4% of the time, Pallas kernels for 0%

profile of v1, /device:TPU:0, one launch (start us, length us, event | category | flops | bytes accessed | tf_op | source)
XLA Modules:
  0.0 400.2 jit_solution(8425989075256754608)
XLA Ops:
  7.3 3.4 collective-permute-start
  11.8 3.1 collective-permute-done.1
  14.9 2.6 collective-permute-start.2
  19.4 2.7 collective-permute-start.4
  24.0 3.7 collective-permute-done.6
  32.0 2.7 collective-permute-start.8
  37.5 2.7 collective-permute-start.10
  42.1 2.7 collective-permute-start.12
  47.0 3.3 collective-permute-done.14
  55.0 2.7 collective-permute-start.16
  60.2 2.7 collective-permute-start.18
  64.9 2.7 collective-permute-start.20
  69.8 3.3 collective-permute-done.22
  80.3 2.7 collective-permute-done.24
  83.1 2.6 collective-permute-start.25
  89.1 2.7 collective-permute-start.27
  94.3 2.8 collective-permute-start.29
  100.0 4.2 %collective-permute-done.31 = f32[4,64,128]{2,1,0:T(8,128)S(1)} collective-permute-done((f32[4,64,128]{2,1,0:T(8,128)S(1)}, f32[4,64,128]{2,1,0:T(8,128)S(1)}, u32[]{:S(2)}, u32[]{:S(2)}) %collective-permute-start.31) | collective-permute-done | bytes 131104 | tf_op jit(solution)/shard_map/ppermute | solution.py:17
  111.0 2.9 collective-permute-done.33
  113.9 2.6 collective-permute-start.34
  120.0 2.7 collective-permute-start.36
  125.2 2.8 collective-permute-start.38
  130.8 4.2 %collective-permute-done.40 = f32[4,64,128]{2,1,0:T(8,128)S(1)} collective-permute-done((f32[4,64,128]{2,1,0:T(8,128)S(1)}, f32[4,64,128]{2,1,0:T(8,128)S(1)}, u32[]{:S(2)}, u32[]{:S(2)}) %collective-permute-start.40) | collective-permute-done | bytes 131104 | tf_op jit(solution)/shard_map/ppermute | solution.py:17
  139.8 54.7 %all-reduce.5.cloned.1.call-done = f32[512,4,128]{2,1,0:T(4,128)} async-done(((f32[512,4,128]{2,1,0:T(4,128)}), f32[512,4,128]{2,1,0:T(4,128)}) %all-reduce.5.cloned.1.call-update) | async-done | bytes 1048592
  198.0 2.7 collective-permute-done.41
  205.7 2.8 convolution_bitcast_fusion
  208.6 36.0 %reduce-scatter.4.cloned.1.call-done = f32[64,4,128]{2,0,1:T(8,128)} async-done(((f32[512,4,128]{2,0,1:T(8,128)}), f32[64,4,128]{2,0,1:T(8,128)}) %reduce-scatter.4.cloned.1.call-update) | async-done | bytes 131088 | tf_op jit(solution)/shard_map/reduce_scatter | solution.py:75
  247.9 2.9 collective-permute-done.43
  252.3 2.6 collective-permute-done.44
  256.7 55.3 %all-reduce.7.cloned.1.call-done = f32[512,2,128]{2,1,0:T(2,128)} async-done(((f32[512,2,128]{2,1,0:T(2,128)}), f32[512,2,128]{2,1,0:T(2,128)}) %all-reduce.7.cloned.1.call-update) | async-done | bytes 524304
  318.8 33.5 %reduce-scatter.6.cloned.1.call-done = f32[64,2,128]{2,0,1:T(8,128)} async-done(((f32[512,2,128]{2,0,1:T(8,128)}), f32[64,2,128]{2,0,1:T(8,128)}) %reduce-scatter.6.cloned.1.call-update) | async-done | bytes 65552 | tf_op jit(solution)/shard_map/reduce_scatter | solution.py:75
  358.4 33.8 %reduce-scatter.8.cloned.1.call-done = f32[64,1,128]{2,1,0:T(1,128)} async-done(((f32[512,1,128]{2,1,0:T(1,128)}), f32[64,1,128]{2,1,0:T(1,128)}) %reduce-scatter.8.cloned.1.call-update) | async-done | bytes 32784 | tf_op jit(solution)/shard_map/reduce_scatter | solution.py:75
  (192 shorter events, 92.8 us)
Async XLA Ops:
  6.5 188.0 %all-reduce.5.cloned.1.call-start = ((), (), s32[]{:S(2)}) async-start(), calls=%async_computation.6 | async-start | bytes 2097152
  7.3 7.6 %collective-permute-start = (f32[1,64,128]{2,1,0:T(8,128)S(1)}, f32[1,64,128]{2,1,0:T(8,128)S(1)}, u32[]{:S(2)}, u32[]{:S(2)}) collective-permute-start(f32[1,64,128]{2,1,0:T(8,128)S(1)} %slice_bitcast_fusion), channel_id=1, source_target_pairs={{0,7},{1,0},{2,1},{3,2},{4,3},{5,4},{6,5},{7,6},{8,15},{9,8},{10,9... | collective-permute-start | bytes 98312 | tf_op jit(solution)/shard_map/ppermute | solution.py:19
  31.9 4.6 %collective-permute-start.9 = (f32[2,64,128]{2,1,0:T(8,128)S(1)}, f32[2,64,128]{2,1,0:T(8,128)S(1)}, u32[]{:S(2)}, u32[]{:S(2)}) collective-permute-start(f32[2,64,128]{2,1,0:T(8,128)S(1)} %maximum_select_fusion.2), channel_id=1, source_target_pairs={{0,1},{1,2},{2,3},{3,4},{4,5},{5,6},{6,7},{7,0},{8,9},{9,10},{10,1... | collective-permute-start | bytes 196616 | tf_op jit(solution)/shard_map/ppermute | solution.py:17
  32.0 4.8 %collective-permute-start.8 = (f32[2,64,128]{2,1,0:T(8,128)S(1)}, f32[2,64,128]{2,1,0:T(8,128)S(1)}, u32[]{:S(2)}, u32[]{:S(2)}) collective-permute-start(f32[2,64,128]{2,1,0:T(8,128)S(1)} %maximum_select_fusion.2), channel_id=1, source_target_pairs={{0,7},{1,0},{2,1},{3,2},{4,3},{5,4},{6,5},{7,6},{8,15},{9,8},{10,9... | collective-permute-start | bytes 196616 | tf_op jit(solution)/shard_map/ppermute | solution.py:19
  36.5 4.6 %collective-permute-start.11 = (f32[2,64,128]{2,1,0:T(8,128)S(1)}, f32[2,64,128]{2,1,0:T(8,128)S(1)}, u32[]{:S(2)}, u32[]{:S(2)}) collective-permute-start(f32[2,64,128]{2,1,0:T(8,128)S(1)} %collective-permute-done.9), channel_id=1, source_target_pairs={{0,1},{1,2},{2,3},{3,4},{4,5},{5,6},{6,7},{7,0},{8,9},{9,10},{10,1... | collective-permute-start | bytes 196616 | tf_op jit(solution)/shard_map/ppermute | solution.py:17
  37.5 4.6 %collective-permute-start.10 = (f32[2,64,128]{2,1,0:T(8,128)S(1)}, f32[2,64,128]{2,1,0:T(8,128)S(1)}, u32[]{:S(2)}, u32[]{:S(2)}) collective-permute-start(f32[2,64,128]{2,1,0:T(8,128)S(1)} %collective-permute-done.8), channel_id=1, source_target_pairs={{0,7},{1,0},{2,1},{3,2},{4,3},{5,4},{6,5},{7,6},{8,15},{9,8},{10,9... | collective-permute-start | bytes 196616 | tf_op jit(solution)/shard_map/ppermute | solution.py:19
  41.1 4.6 %collective-permute-start.13 = (f32[2,64,128]{2,1,0:T(8,128)S(1)}, f32[2,64,128]{2,1,0:T(8,128)S(1)}, u32[]{:S(2)}, u32[]{:S(2)}) collective-permute-start(f32[2,64,128]{2,1,0:T(8,128)S(1)} %collective-permute-done.11), channel_id=1, source_target_pairs={{0,1},{1,2},{2,3},{3,4},{4,5},{5,6},{6,7},{7,0},{8,9},{9,10},{10,1... | collective-permute-start | bytes 196616 | tf_op jit(solution)/shard_map/ppermute | solution.py:17
  54.6 4.6 %collective-permute-start.17 = (f32[2,64,128]{2,1,0:T(8,128)S(1)}, f32[2,64,128]{2,1,0:T(8,128)S(1)}, u32[]{:S(2)}, u32[]{:S(2)}) collective-permute-start(f32[2,64,128]{2,1,0:T(8,128)S(1)} %maximum_select_fusion.3), channel_id=1, source_target_pairs={{0,1},{1,2},{2,3},{3,4},{4,5},{5,6},{6,7},{7,0},{8,9},{9,10},{10,1... | collective-permute-start | bytes 196616 | tf_op jit(solution)/shard_map/ppermute | solution.py:17
  55.0 4.6 %collective-permute-start.16 = (f32[2,64,128]{2,1,0:T(8,128)S(1)}, f32[2,64,128]{2,1,0:T(8,128)S(1)}, u32[]{:S(2)}, u32[]{:S(2)}) collective-permute-start(f32[2,64,128]{2,1,0:T(8,128)S(1)} %maximum_select_fusion.3), channel_id=1, source_target_pairs={{0,7},{1,0},{2,1},{3,2},{4,3},{5,4},{6,5},{7,6},{8,15},{9,8},{10,9... | collective-permute-start | bytes 196616 | tf_op jit(solution)/shard_map/ppermute | solution.py:19
  60.2 4.6 %collective-permute-start.18 = (f32[2,64,128]{2,1,0:T(8,128)S(1)}, f32[2,64,128]{2,1,0:T(8,128)S(1)}, u32[]{:S(2)}, u32[]{:S(2)}) collective-permute-start(f32[2,64,128]{2,1,0:T(8,128)S(1)} %collective-permute-done.16), channel_id=1, source_target_pairs={{0,7},{1,0},{2,1},{3,2},{4,3},{5,4},{6,5},{7,6},{8,15},{9,8},{10,9... | collective-permute-start | bytes 196616 | tf_op jit(solution)/shard_map/ppermute | solution.py:19
  77.8 5.2 %collective-permute-start.24 = (f32[2,64,128]{2,1,0:T(8,128)S(1)}, f32[2,64,128]{2,1,0:T(8,128)S(1)}, u32[]{:S(2)}, u32[]{:S(2)}) collective-permute-start(f32[2,64,128]{2,1,0:T(8,128)S(1)} %maximum_select_fusion.4), channel_id=1, source_target_pairs={{0,16},{8,24},{16,0},{24,8},{1,17},{9,25},{17,1},{25,9},{2,18},{10... | collective-permute-start | bytes 196616 | tf_op jit(solution)/shard_map/ppermute | solution.py:28
  83.0 5.3 %collective-permute-start.26 = (f32[4,64,128]{2,1,0:T(8,128)S(1)}, f32[4,64,128]{2,1,0:T(8,128)S(1)}, u32[]{:S(2)}, u32[]{:S(2)}) collective-permute-start(f32[4,64,128]{2,1,0:T(8,128)S(1)} %maximum_select_fusion), channel_id=1, source_target_pairs={{0,1},{1,2},{2,3},{3,4},{4,5},{5,6},{6,7},{7,0},{8,9},{9,10},{10,1... | collective-permute-start | bytes 393224 | tf_op jit(solution)/shard_map/ppermute | solution.py:17
  83.1 5.7 %collective-permute-start.25 = (f32[4,64,128]{2,1,0:T(8,128)S(1)}, f32[4,64,128]{2,1,0:T(8,128)S(1)}, u32[]{:S(2)}, u32[]{:S(2)}) collective-permute-start(f32[4,64,128]{2,1,0:T(8,128)S(1)} %maximum_select_fusion), channel_id=1, source_target_pairs={{0,7},{1,0},{2,1},{3,2},{4,3},{5,4},{6,5},{7,6},{8,15},{9,8},{10,9... | collective-permute-start | bytes 393224 | tf_op jit(solution)/shard_map/ppermute | solution.py:19
  88.4 5.3 %collective-permute-start.28 = (f32[4,64,128]{2,1,0:T(8,128)S(1)}, f32[4,64,128]{2,1,0:T(8,128)S(1)}, u32[]{:S(2)}, u32[]{:S(2)}) collective-permute-start(f32[4,64,128]{2,1,0:T(8,128)S(1)} %collective-permute-done.26), channel_id=1, source_target_pairs={{0,1},{1,2},{2,3},{3,4},{4,5},{5,6},{6,7},{7,0},{8,9},{9,10},{10,1... | collective-permute-start | bytes 393224 | tf_op jit(solution)/shard_map/ppermute | solution.py:17
  89.1 5.2 %collective-permute-start.27 = (f32[4,64,128]{2,1,0:T(8,128)S(1)}, f32[4,64,128]{2,1,0:T(8,128)S(1)}, u32[]{:S(2)}, u32[]{:S(2)}) collective-permute-start(f32[4,64,128]{2,1,0:T(8,128)S(1)} %collective-permute-done.25), channel_id=1, source_target_pairs={{0,7},{1,0},{2,1},{3,2},{4,3},{5,4},{6,5},{7,6},{8,15},{9,8},{10,9... | collective-permute-start | bytes 393224 | tf_op jit(solution)/shard_map/ppermute | solution.py:19
  93.7 5.3 %collective-permute-start.30 = (f32[4,64,128]{2,1,0:T(8,128)S(1)}, f32[4,64,128]{2,1,0:T(8,128)S(1)}, u32[]{:S(2)}, u32[]{:S(2)}) collective-permute-start(f32[4,64,128]{2,1,0:T(8,128)S(1)} %collective-permute-done.28), channel_id=1, source_target_pairs={{0,1},{1,2},{2,3},{3,4},{4,5},{5,6},{6,7},{7,0},{8,9},{9,10},{10,1... | collective-permute-start | bytes 393224 | tf_op jit(solution)/shard_map/ppermute | solution.py:17
  94.3 5.3 %collective-permute-start.29 = (f32[4,64,128]{2,1,0:T(8,128)S(1)}, f32[4,64,128]{2,1,0:T(8,128)S(1)}, u32[]{:S(2)}, u32[]{:S(2)}) collective-permute-start(f32[4,64,128]{2,1,0:T(8,128)S(1)} %collective-permute-done.27), channel_id=1, source_target_pairs={{0,7},{1,0},{2,1},{3,2},{4,3},{5,4},{6,5},{7,6},{8,15},{9,8},{10,9... | collective-permute-start | bytes 393224 | tf_op jit(solution)/shard_map/ppermute | solution.py:19
  99.0 5.3 %collective-permute-start.31 = (f32[4,64,128]{2,1,0:T(8,128)S(1)}, f32[4,64,128]{2,1,0:T(8,128)S(1)}, u32[]{:S(2)}, u32[]{:S(2)}) collective-permute-start(f32[4,64,128]{2,1,0:T(8,128)S(1)} %collective-permute-done.30), channel_id=1, source_target_pairs={{0,1},{1,2},{2,3},{3,4},{4,5},{5,6},{6,7},{7,0},{8,9},{9,10},{10,1... | collective-permute-start | bytes 393224 | tf_op jit(solution)/shard_map/ppermute | solution.py:17
  108.6 5.2 %collective-permute-start.33 = (f32[2,64,128]{2,1,0:T(8,128)S(1)}, f32[2,64,128]{2,1,0:T(8,128)S(1)}, u32[]{:S(2)}, u32[]{:S(2)}) collective-permute-start(f32[2,64,128]{2,1,0:T(8,128)S(1)} %maximum_select_fusion.5), channel_id=1, source_target_pairs={{0,16},{8,24},{16,0},{24,8},{1,17},{9,25},{17,1},{25,9},{2,18},{10... | collective-permute-start | bytes 196616 | tf_op jit(solution)/shard_map/ppermute | solution.py:28
  113.9 5.3 %collective-permute-start.35 = (f32[4,64,128]{2,1,0:T(8,128)S(1)}, f32[4,64,128]{2,1,0:T(8,128)S(1)}, u32[]{:S(2)}, u32[]{:S(2)}) collective-permute-start(f32[4,64,128]{2,1,0:T(8,128)S(1)} %maximum_select_fusion.1), channel_id=1, source_target_pairs={{0,1},{1,2},{2,3},{3,4},{4,5},{5,6},{6,7},{7,0},{8,9},{9,10},{10,1... | collective-permute-start | bytes 393224 | tf_op jit(solution)/shard_map/ppermute | solution.py:17
  113.9 5.7 %collective-permute-start.34 = (f32[4,64,128]{2,1,0:T(8,128)S(1)}, f32[4,64,128]{2,1,0:T(8,128)S(1)}, u32[]{:S(2)}, u32[]{:S(2)}) collective-permute-start(f32[4,64,128]{2,1,0:T(8,128)S(1)} %maximum_select_fusion.1), channel_id=1, source_target_pairs={{0,7},{1,0},{2,1},{3,2},{4,3},{5,4},{6,5},{7,6},{8,15},{9,8},{10,9... | collective-permute-start | bytes 393224 | tf_op jit(solution)/shard_map/ppermute | solution.py:19
  119.2 5.3 %collective-permute-start.37 = (f32[4,64,128]{2,1,0:T(8,128)S(1)}, f32[4,64,128]{2,1,0:T(8,128)S(1)}, u32[]{:S(2)}, u32[]{:S(2)}) collective-permute-start(f32[4,64,128]{2,1,0:T(8,128)S(1)} %collective-permute-done.35), channel_id=1, source_target_pairs={{0,1},{1,2},{2,3},{3,4},{4,5},{5,6},{6,7},{7,0},{8,9},{9,10},{10,1... | collective-permute-start | bytes 393224 | tf_op jit(solution)/shard_map/ppermute | solution.py:17
  120.0 5.2 %collective-permute-start.36 = (f32[4,64,128]{2,1,0:T(8,128)S(1)}, f32[4,64,128]{2,1,0:T(8,128)S(1)}, u32[]{:S(2)}, u32[]{:S(2)}) collective-permute-start(f32[4,64,128]{2,1,0:T(8,128)S(1)} %collective-permute-done.34), channel_id=1, source_target_pairs={{0,7},{1,0},{2,1},{3,2},{4,3},{5,4},{6,5},{7,6},{8,15},{9,8},{10,9... | collective-permute-start | bytes 393224 | tf_op jit(solution)/shard_map/ppermute | solution.py:19
  124.5 5.3 %collective-permute-start.39 = (f32[4,64,128]{2,1,0:T(8,128)S(1)}, f32[4,64,128]{2,1,0:T(8,128)S(1)}, u32[]{:S(2)}, u32[]{:S(2)}) collective-permute-start(f32[4,64,128]{2,1,0:T(8,128)S(1)} %collective-permute-done.37), channel_id=1, source_target_pairs={{0,1},{1,2},{2,3},{3,4},{4,5},{5,6},{6,7},{7,0},{8,9},{9,10},{10,1... | collective-permute-start | bytes 393224 | tf_op jit(solution)/shard_map/ppermute | solution.py:17
  125.2 5.3 %collective-permute-start.38 = (f32[4,64,128]{2,1,0:T(8,128)S(1)}, f32[4,64,128]{2,1,0:T(8,128)S(1)}, u32[]{:S(2)}, u32[]{:S(2)}) collective-permute-start(f32[4,64,128]{2,1,0:T(8,128)S(1)} %collective-permute-done.36), channel_id=1, source_target_pairs={{0,7},{1,0},{2,1},{3,2},{4,3},{5,4},{6,5},{7,6},{8,15},{9,8},{10,9... | collective-permute-start | bytes 393224 | tf_op jit(solution)/shard_map/ppermute | solution.py:19
  129.8 5.3 %collective-permute-start.40 = (f32[4,64,128]{2,1,0:T(8,128)S(1)}, f32[4,64,128]{2,1,0:T(8,128)S(1)}, u32[]{:S(2)}, u32[]{:S(2)}) collective-permute-start(f32[4,64,128]{2,1,0:T(8,128)S(1)} %collective-permute-done.39), channel_id=1, source_target_pairs={{0,1},{1,2},{2,3},{3,4},{4,5},{5,6},{6,7},{7,0},{8,9},{9,10},{10,1... | collective-permute-start | bytes 393224 | tf_op jit(solution)/shard_map/ppermute | solution.py:17
  137.9 106.7 %reduce-scatter.4.cloned.1.call-start = ((), (), s32[]{:S(2)}) async-start(), calls=%async_computation.3 | async-start | bytes 1179648 | tf_op jit(solution)/shard_map/reduce_scatter | solution.py:75
  195.5 5.2 %collective-permute-start.41 = (f32[64,2,128]{2,1,0:T(2,128)S(1)}, f32[64,2,128]{2,1,0:T(2,128)S(1)}, u32[]{:S(2)}, u32[]{:S(2)}) collective-permute-start(f32[64,2,128]{2,1,0:T(2,128)S(1)} %constant_dynamic-slice_fusion.6), channel_id=1, source_target_pairs={{0,16},{8,24},{16,0},{24,8},{1,17},{9,25},{17,1},{25,9},{2,18},{10... | collective-permute-start | bytes 196616 | tf_op jit(solution)/shard_map/ppermute | solution.py:28
  208.5 103.5 %all-reduce.7.cloned.1.call-start = ((), (), s32[]{:S(2)}) async-start(), calls=%async_computation.7 | async-start | bytes 1048576
  245.5 5.3 %collective-permute-start.43 = (f32[64,2,128]{2,0,1:T(8,128)S(1)}, f32[64,2,128]{2,0,1:T(8,128)S(1)}, u32[]{:S(2)}, u32[]{:S(2)}) collective-permute-start(f32[64,2,128]{2,0,1:T(8,128)S(1)} %constant_dynamic-slice_fusion.4), channel_id=1, source_target_pairs={{0,16},{8,24},{16,0},{24,8},{1,17},{9,25},{17,1},{25,9},{2,18},{10... | collective-permute-start | bytes 196616 | tf_op jit(solution)/shard_map/ppermute | solution.py:28
  256.5 95.9 %reduce-scatter.6.cloned.1.call-start = ((), (), s32[]{:S(2)}) async-start(), calls=%async_computation.4 | async-start | bytes 589824 | tf_op jit(solution)/shard_map/reduce_scatter | solution.py:75
  318.8 73.4 %reduce-scatter.8.cloned.1.call-start = ((), (), s32[]{:S(2)}) async-start(), calls=%async_computation.5 | async-start | bytes 294912 | tf_op jit(solution)/shard_map/reduce_scatter | solution.py:75
  (31 other events, 163.0 us)
Sparse Core Ops, SparseCore 0:
  138.0 56.4 all-reduce.4
  208.7 35.9 reduce-scatter.3
  256.6 55.3 all-reduce.6
  318.9 33.4 reduce-scatter.5
  358.5 33.6 reduce-scatter.7
